TPU v7x, 32 devices: a whole 2x2x4 slice. The times are simulated.
32 devices in a mesh: fsdp: 2 (over x), ctx: 4 (over z), tp: 4 (over y, core).
Axes of the slice: x: 2, y: 2, z: 4, core: 2. Of those that a mesh axis runs over, the one named last changes fastest.
Arguments:
- tokens: bfloat16 [8192, 1024], P(('fsdp', 'ctx')), may hold values from -6 to 6
- w_qkv: bfloat16 [3, 1024, 1024], P(None, 'fsdp', 'tp'), may hold values from -0.25 to 0.25
- w_out: bfloat16 [1024, 1024], P('tp', 'fsdp'), may hold values from -0.75 to 0.75
- w_up: bfloat16 [1024, 4096], P('fsdp', 'tp'), may hold values from -0.1875 to 0.1875
- w_down: bfloat16 [4096, 1024], P('tp', 'fsdp'), may hold values from -0.09375 to 0.09375
- gains: bfloat16 [2, 1024], P(None, 'fsdp'), may hold values from 0.5 to 1.5
- shifts: bfloat16 [2, 1024], P(None, 'fsdp'), may hold values from -3 to 3
- lengths: int32 [2, 3], P('fsdp'), may hold values from 256 to 2048, as said below
- out_grad: bfloat16 [8192, 1024], P(('fsdp', 'ctx')), may hold values from -6 to 6
Outputs:
- out: bfloat16 [8192, 1024], P(('fsdp', 'ctx'))
- input_grad: bfloat16 [8192, 1024], P(('fsdp', 'ctx'))
- grad_qkv: float32 [3, 1024, 1024], P(None, 'fsdp', 'tp')
- grad_out: float32 [1024, 1024], P('tp', 'fsdp')
- grad_up: float32 [1024, 4096], P('fsdp', 'tp')
- grad_down: float32 [4096, 1024], P('tp', 'fsdp')
- grad_gains: float32 [2, 1024], P(None, 'fsdp')
- grad_shifts: float32 [2, 1024], P(None, 'fsdp')
Inputs may be any that keep to these rules, and one draw needn't show every extreme that they name: `lengths`: in each row one sequence has exactly 2048 tokens and the others 2048 // 8 to 1024; sequences lie end to end from the pack's first slot, and the slots after them up to 4096 are padding.
All inputs are finite; a program needn't handle non-finite values.
Results may differ from a plain program's by a relative error of at most 0.014.
The roundings to bfloat16 on the way count: a program that leaves them out, or rounds other values in their place, can miss the bound.
Values may be sent and summed in bfloat16 or wider, within the bound.
No kernel may reach another device: no remote copies, remote signals or barrier semaphores. Data moves between devices by JAX's collectives and lax.ppermute only.
A program may use at most 192 MiB of HBM per device.

v0:
```python
import math
import jax
import jax.numpy as jnp
from jax import lax
from jax.sharding import PartitionSpec as P

HEAD_DIM = 64
SEQS = 3
norm_eps = 1e-12
masked_low = -1e30


def layer_norm(rows, gain, shift):
    centre = rows - jnp.mean(rows, axis=-1, keepdims=True)
    spread = jnp.mean(centre * centre, axis=-1, keepdims=True)
    return centre * lax.rsqrt(spread + norm_eps) * gain + shift


def exact_gelu(values):
    return jax.nn.gelu(values, approximate=False)


def contract_rows(left, right):
    return lax.dot_general(
        left, right, (((0,), (0,)), ((), ())), preferred_element_type=jnp.float32
    )


def contract_cols(left, right):
    return lax.dot_general(
        left, right, (((1,), (1,)), ((), ())), preferred_element_type=jnp.float32
    )


def tp_total(terms):
    return lax.psum(terms, "tp")


def segment_of(lengths_row, total):
    seq_ends = jnp.cumsum(lengths_row)
    positions = jnp.arange(total, dtype=jnp.int32)
    return jnp.sum((positions[:, None] >= seq_ends[None, :]).astype(jnp.int32), axis=1)


def score_block(query_block, seg_block, key_heads, segments):
    raw_scores = jnp.einsum(
        "qhd,khd->hqk", query_block, key_heads, preferred_element_type=jnp.float32
    )
    allowed = (seg_block[:, None] == segments[None, :]) & (segments[None, :] < SEQS)
    return (raw_scores * (1.0 / math.sqrt(HEAD_DIM)), allowed)


def attend_forward(query_heads, seg_mine, key_heads, value_heads, segments):

    def one_block(inputs):
        query_block, seg_block = inputs
        scores, allowed = score_block(query_block, seg_block, key_heads, segments)
        has_key = jnp.any(allowed, axis=1)
        masked = jnp.where(allowed[None], scores, masked_low)
        row_max = jnp.where(has_key[None, :, None], jnp.max(masked, axis=2, keepdims=True), 0.0)
        exp_terms = jnp.where(allowed[None], jnp.exp(masked - row_max), 0.0)
        denominator = (
            jnp.sum(exp_terms, axis=2, keepdims=True)
            + (1.0 - has_key.astype(jnp.float32))[None, :, None]
        )
        attn_probs = (exp_terms / denominator).astype(jnp.bfloat16)
        context = jnp.einsum(
            "hqk,khd->qhd", attn_probs, value_heads, preferred_element_type=jnp.float32
        )
        log_total = row_max[:, :, 0] + jnp.log(denominator[:, :, 0])
        return (context.astype(jnp.bfloat16), log_total)

    return lax.map(one_block, (query_heads, seg_mine))


def attend_backward(
    query_heads, seg_mine, grad_heads, log_totals, key_heads, value_heads, segments
):
    score_scale = 1.0 / math.sqrt(HEAD_DIM)
    zero_keys = jnp.zeros(key_heads.shape, jnp.float32)

    def one_block(carry, inputs):
        key_grad, value_grad = carry
        query_block, seg_block, grad_block, log_block = inputs
        scores, allowed = score_block(query_block, seg_block, key_heads, segments)
        attn_probs = jnp.where(allowed[None], jnp.exp(scores - log_block[:, :, None]), 0.0)
        probs_low = attn_probs.astype(jnp.bfloat16)
        grad_probs = jnp.einsum(
            "qhd,khd->hqk", grad_block, value_heads, preferred_element_type=jnp.float32
        )
        row_delta = jnp.sum(attn_probs * grad_probs, axis=2, keepdims=True)
        grad_scores = (attn_probs * (grad_probs - row_delta) * score_scale).astype(jnp.bfloat16)
        query_grad = jnp.einsum(
            "hqk,khd->qhd", grad_scores, key_heads, preferred_element_type=jnp.float32
        )
        key_grad = key_grad + jnp.einsum(
            "hqk,qhd->khd", grad_scores, query_block, preferred_element_type=jnp.float32
        )
        value_grad = value_grad + jnp.einsum(
            "hqk,qhd->khd", probs_low, grad_block, preferred_element_type=jnp.float32
        )
        return ((key_grad, value_grad), query_grad)

    return lax.scan(
        one_block, (zero_keys, zero_keys), (query_heads, seg_mine, grad_heads, log_totals)
    )


def body(tokens, w_qkv, w_out, w_up, w_down, gains, shifts, lengths, out_grad):
    full_qkv, full_out, full_up, full_down, full_gains, full_shifts = (
        lax.all_gather(w_qkv, "fsdp", axis=1, tiled=True),
        lax.all_gather(w_out, "fsdp", axis=1, tiled=True),
        lax.all_gather(w_up, "fsdp", axis=0, tiled=True),
        lax.all_gather(w_down, "fsdp", axis=1, tiled=True),
        lax.all_gather(gains, "fsdp", axis=1, tiled=True),
        lax.all_gather(shifts, "fsdp", axis=1, tiled=True),
    )
    tok_rows = tokens.shape[0]
    local_width = full_qkv.shape[2]
    local_heads = local_width // HEAD_DIM
    block_rows = min(512, tok_rows)
    block_count = tok_rows // block_rows
    pack_rows = tok_rows * lax.axis_size("ctx")
    segments = segment_of(lengths[0], pack_rows)
    seg_mine = lax.dynamic_slice_in_dim(
        segments, lax.axis_index("ctx") * tok_rows, tok_rows
    ).reshape(block_count, block_rows)
    residual_in = tokens.astype(jnp.float32)
    projected = jnp.einsum(
        "td,sdc->stc", tokens, full_qkv, preferred_element_type=jnp.float32
    ).astype(jnp.bfloat16)
    key_rows, value_rows = (
        lax.all_gather(projected[1], "ctx", axis=0, tiled=True),
        lax.all_gather(projected[2], "ctx", axis=0, tiled=True),
    )
    key_heads = key_rows.reshape(pack_rows, local_heads, HEAD_DIM)
    value_heads = value_rows.reshape(pack_rows, local_heads, HEAD_DIM)
    query_heads = projected[0].reshape(block_count, block_rows, local_heads, HEAD_DIM)
    context_blocks, log_totals = attend_forward(
        query_heads, seg_mine, key_heads, value_heads, segments
    )
    context = context_blocks.reshape(tok_rows, local_width)
    attn_terms = jnp.dot(context, full_out, preferred_element_type=jnp.float32)
    resid_rows = residual_in + tp_total(attn_terms)
    grad_rows = out_grad.astype(jnp.float32)
    gain_full = full_gains.astype(jnp.float32)
    shift_full = full_shifts.astype(jnp.float32)
    hidden, norm_first = jax.vjp(layer_norm, resid_rows, gain_full[0], shift_full[0])
    hidden_part = hidden.astype(jnp.bfloat16)
    pre_act = jnp.dot(hidden_part, full_up, preferred_element_type=jnp.float32)
    activated, gelu_back = jax.vjp(exact_gelu, pre_act)
    act_low = activated.astype(jnp.bfloat16)
    ffn_terms = jnp.dot(act_low, full_down, preferred_element_type=jnp.float32)
    ffn_rows = tp_total(ffn_terms)
    result, norm_second = jax.vjp(layer_norm, hidden + ffn_rows, gain_full[1], shift_full[1])
    grad_mid, gain_second, shift_second = norm_second(grad_rows)
    mid_part = grad_mid.astype(jnp.bfloat16)
    result_part = result.astype(jnp.bfloat16)
    back_qkv, back_out, back_up, back_down = (
        lax.all_gather(w_qkv, "fsdp", axis=1, tiled=True),
        lax.all_gather(w_out, "fsdp", axis=1, tiled=True),
        lax.all_gather(w_up, "fsdp", axis=0, tiled=True),
        lax.all_gather(w_down, "fsdp", axis=1, tiled=True),
    )
    down_grad = contract_rows(act_low, mid_part)
    act_grad = contract_cols(mid_part, back_down)
    (pre_grad,) = gelu_back(act_grad)
    pre_low = pre_grad.astype(jnp.bfloat16)
    up_grad = contract_rows(hidden_part, pre_low)
    hidden_terms = contract_cols(pre_low, back_up)
    hidden_grad = grad_mid + tp_total(hidden_terms)
    resid_grad, gain_first, shift_first = norm_first(hidden_grad)
    attn_part = resid_grad.astype(jnp.bfloat16)
    out_proj_grad = contract_rows(context, attn_part)
    context_grad = contract_cols(attn_part, back_out).astype(jnp.bfloat16)
    grad_heads = context_grad.reshape(block_count, block_rows, local_heads, HEAD_DIM)
    (key_grad, value_grad), query_grad = attend_backward(
        query_heads, seg_mine, grad_heads, log_totals, key_heads, value_heads, segments
    )
    key_mine, value_mine = (
        lax.psum_scatter(
            key_grad.reshape(pack_rows, local_width), "ctx", scatter_dimension=0, tiled=True
        ),
        lax.psum_scatter(
            value_grad.reshape(pack_rows, local_width), "ctx", scatter_dimension=0, tiled=True
        ),
    )
    proj_grad = jnp.stack(
        [
            query_grad.reshape(tok_rows, local_width).astype(jnp.bfloat16),
            key_mine.astype(jnp.bfloat16),
            value_mine.astype(jnp.bfloat16),
        ]
    )
    qkv_grad = jnp.einsum("td,stc->sdc", tokens, proj_grad, preferred_element_type=jnp.float32)
    input_part = jnp.einsum("stc,sdc->td", proj_grad, back_qkv, preferred_element_type=jnp.float32)
    input_grad = (resid_grad + tp_total(input_part)).astype(jnp.bfloat16)
    gain_grad = jnp.stack([gain_first, gain_second])
    shift_grad = jnp.stack([shift_first, shift_second])
    qkv_grad, out_proj_grad, up_grad, down_grad, gain_grad, shift_grad = (
        lax.psum_scatter(qkv_grad, "fsdp", scatter_dimension=1, tiled=True),
        lax.psum_scatter(out_proj_grad, "fsdp", scatter_dimension=1, tiled=True),
        lax.psum_scatter(up_grad, "fsdp", scatter_dimension=0, tiled=True),
        lax.psum_scatter(down_grad, "fsdp", scatter_dimension=1, tiled=True),
        lax.psum_scatter(gain_grad, "fsdp", scatter_dimension=1, tiled=True),
        lax.psum_scatter(shift_grad, "fsdp", scatter_dimension=1, tiled=True),
    )
    qkv_grad, out_proj_grad, up_grad, down_grad, gain_grad, shift_grad = lax.psum(
        (qkv_grad, out_proj_grad, up_grad, down_grad, gain_grad, shift_grad), "ctx"
    )
    return (
        result_part,
        input_grad,
        qkv_grad,
        out_proj_grad,
        up_grad,
        down_grad,
        gain_grad,
        shift_grad,
    )


def solution(mesh):
    return jax.shard_map(
        body,
        mesh=mesh,
        in_specs=(
            P(("fsdp", "ctx"), None),
            P(None, "fsdp", "tp"),
            P("tp", "fsdp"),
            P("fsdp", "tp"),
            P("tp", "fsdp"),
            P(None, "fsdp"),
            P(None, "fsdp"),
            P("fsdp", None),
            P(("fsdp", "ctx"), None),
        ),
        out_specs=(
            P(("fsdp", "ctx"), None),
            P(("fsdp", "ctx"), None),
            P(None, "fsdp", "tp"),
            P("tp", "fsdp"),
            P("fsdp", "tp"),
            P("tp", "fsdp"),
            P(None, "fsdp"),
            P(None, "fsdp"),
        ),
        check_vma=False,
    )
```

profile of v0, /device:TPU:0, one launch (start us, length us, event | category | flops | bytes accessed | tf_op | source)
XLA Modules:
  0.0 1667.1 jit_solution(5852999273512513464)
XLA Ops:
  9.6 30.5 %all-gather.8.cloned.1.call-done = bf16[3,1024,256]{1,2,0:T(8,128)(2,1)} async-done(((bf16[3,512,256]{1,2,0:T(8,128)(2,1)}), bf16[3,1024,256]{1,2,0:T(8,128)(2,1)}) %all-gather.8.cloned.1.call-update) | async-done | bytes 1572880 | tf_op jit(solution)/shard_map/all_gather | solution.py:111
  46.3 9.0 all_gather.31
  55.7 35.5 %all-gather.14.cloned.1.call-done = bf16[1,4096,256]{1,2,0:T(8,128)(2,1)} async-done(((bf16[1,1024,256]{1,2,0:T(8,128)(2,1)}), bf16[1,4096,256]{1,2,0:T(8,128)(2,1)}) %all-gather.14.cloned.1.call-update) | async-done | bytes 2097168 | tf_op jit(solution)/shard_map/all_gather | solution.py:133
  91.2 46.9 %all-gather.16.cloned.1.call-done = bf16[1,4096,256]{1,2,0:T(8,128)(2,1)} async-done(((bf16[1,1024,256]{1,2,0:T(8,128)(2,1)}), bf16[1,4096,256]{1,2,0:T(8,128)(2,1)}) %all-gather.16.cloned.1.call-update) | async-done | bytes 2097168 | tf_op jit(solution)/shard_map/all_gather | solution.py:134
  138.0 99.9 %while.27 = (s32[]{:T(128)}, bf16[2,512,4,64]{1,3,2,0:T(8,128)(2,1)}, f32[2,4,512]{2,1,0:T(4,128)S(1)}, s32[2,512]{1,0:T(2,128)S(1)}, s32[4096]{0:T(1024)S(1)}, ...) while((s32[]{:T(128)}, ...), condition=%wide.region_6.7_spmd, body=%wide.region_2.6_spmd.sunk | while | flops 2271357440 | bytes 113924704 | solution.py:73
  140.3 15.8 fusion.181
  156.1 15.6 fusion.182
  171.8 16.2 fusion.183
  190.3 15.8 fusion.181
  206.1 15.6 fusion.182
  221.7 16.2 fusion.183
  248.7 4.6 all_gather.33
  253.3 74.2 %all-reduce.8.cloned.1.call-done = f32[1024,1024]{1,0:T(8,128)} async-done(((f32[1024,1024]{1,0:T(8,128)}), f32[1024,1024]{1,0:T(8,128)}) %all-reduce.8.cloned.1.call-update) | async-done | bytes 4194320 | tf_op jit(solution)/shard_map/psum | solution.py:36
  332.7 29.5 %all-gather.10.cloned.1.call-done = bf16[1024,1024]{1,0:T(8,128)(2,1)} async-done(((bf16[512,1024]{1,0:T(8,128)(2,1)}), bf16[1024,1024]{1,0:T(8,128)(2,1)}) %all-gather.10.cloned.1.call-update) | async-done | bytes 2097168 | tf_op jit(solution)/shard_map/all_gather | solution.py:113
  362.2 15.5 multiply_convert_fusion.1
  377.7 19.1 %all-gather.12.cloned.1.call-done = bf16[1024,1024]{1,0:T(8,128)(2,1)} async-done(((bf16[1024,512]{1,0:T(8,128)(2,1)}), bf16[1024,1024]{1,0:T(8,128)(2,1)}) %all-gather.12.cloned.1.call-update) | async-done | bytes 2097168 | tf_op jit(solution)/shard_map/all_gather | solution.py:114
  396.9 6.5 fusion.135
  403.8 85.2 %all-reduce.10.cloned.1.call-done = f32[1024,1024]{1,0:T(8,128)} async-done(((f32[1024,1024]{1,0:T(8,128)}), f32[1024,1024]{1,0:T(8,128)}) %all-reduce.10.cloned.1.call-update) | async-done | bytes 4194320 | tf_op jit(solution)/shard_map/psum | solution.py:36
  513.4 85.7 %all-reduce.12.cloned.1.call-done = f32[1024,1024]{1,0:T(8,128)} async-done(((f32[1024,1024]{1,0:T(8,128)}), f32[1024,1024]{1,0:T(8,128)}) %all-reduce.12.cloned.1.call-update) | async-done | bytes 4194320 | tf_op jit(solution)/shard_map/psum | solution.py:36
  599.1 6.4 multiply_reduce_fusion.1
  615.2 341.7 %while.28 = (s32[]{:T(128)}, f32[4096,4,64]{0,2,1:T(8,128)}, f32[4096,4,64]{0,2,1:T(8,128)}, bf16[2,512,4,64]{1,3,2,0:T(8,128)(2,1)}, bf16[2,512,4,64]{1,3,2,0:T...) while((s32[]{:T(128)}, f32[4096,4,64]{0,2,1:T(8,128)}, ...), condition=%wide.region_20.21_spmd.clone, body=%wide.region_18.20_spmd.clone.sunk | while | flops 5595217920 | bytes 414817440 | solution.py:104
  618.2 13.1 fusion.196
  631.3 13.1 fusion.195
  644.4 63.5 %fusion.197 = f32[4096,4,64]{0,2,1:T(8,128)} fusion(f32[4,512,4096]{2,1,0:T(8,128)} %fusion.195, f32[4,512,4096]{2,1,0:T(8,128)} %fusion.196, f32[4,512]{1,0:T(4,128)S(1)} %dynamic-slice_bitcast_fusion.2, pred[512,4096]{1,0:T(8,128)(4,1)} %compare_and_fusion.3, f32[4096,4,64]{0,2,1:T(8,128)} %get-tuple-element.498, pred[]{:T(512)S(6)} %compare.3, ...), kind=kOutput, calls=%fused_computation.48.clone.1 | convolution fusion | flops 1168119808 | bytes 147079680 | tf_op jit(solution)/shard_map/while/body/eval_jaxpr/hqk,qhd->khd/dot_general | solution.py:96
  708.0 60.0 %fusion.199 = bf16[2,512,4,64]{1,3,2,0:T(8,128)(2,1)} fusion(bf16[2,512,4,64]{1,3,2,0:T(8,128)(2,1)} %get-tuple-element.500, s32[]{:T(128)} %get-tuple-element.497, bf16[4096,4,64]{0,2,1:T(8,128)(2,1)S(1)} %get-tuple-element.517, f32[4,512,4096]{2,1,0:T(8,128)} %fusion.195, f32[4,512,4096]{2,1,0:T(8,128)} %fusion.196, ...), kind=kOutput, calls=%fused_computation.52.clone.1 | convolution fusion | flops 1166022656 | bytes 141050368 | tf_op jit(solution)/shard_map/while/body/eval_jaxpr/hqk,khd->qhd/dot_general | solution.py:93
  767.9 17.3 %fusion.198 = f32[4096,4,64]{0,2,1:T(8,128)} fusion(f32[4,512,4096]{2,1,0:T(8,128)} %fusion.196, f32[4,512]{1,0:T(4,128)S(1)} %dynamic-slice_bitcast_fusion.2, pred[512,4096]{1,0:T(8,128)(4,1)} %compare_and_fusion.3, f32[4096,4,64]{0,2,1:T(8,128)} %get-tuple-element.499, pred[]{:T(512)S(6)} %compare.3, ...), kind=kOutput, calls=%fused_computation.50.clone.1 | convolution fusion | flops 1109393408 | bytes 44310532 | tf_op jit(solution)/shard_map/while/body/eval_jaxpr/hqk,qhd->khd/dot_general | solution.py:99
  788.1 13.1 fusion.196
  801.2 13.1 fusion.195
  814.3 64.0 %fusion.197 = f32[4096,4,64]{0,2,1:T(8,128)} fusion(f32[4,512,4096]{2,1,0:T(8,128)} %fusion.195, f32[4,512,4096]{2,1,0:T(8,128)} %fusion.196, f32[4,512]{1,0:T(4,128)S(1)} %dynamic-slice_bitcast_fusion.2, pred[512,4096]{1,0:T(8,128)(4,1)} %compare_and_fusion.3, f32[4096,4,64]{0,2,1:T(8,128)} %get-tuple-element.498, pred[]{:T(512)S(6)} %compare.3, ...), kind=kOutput, calls=%fused_computation.48.clone.1 | convolution fusion | flops 1168119808 | bytes 147079680 | tf_op jit(solution)/shard_map/while/body/eval_jaxpr/hqk,qhd->khd/dot_general | solution.py:96
  878.3 60.0 %fusion.199 = bf16[2,512,4,64]{1,3,2,0:T(8,128)(2,1)} fusion(bf16[2,512,4,64]{1,3,2,0:T(8,128)(2,1)} %get-tuple-element.500, s32[]{:T(128)} %get-tuple-element.497, bf16[4096,4,64]{0,2,1:T(8,128)(2,1)S(1)} %get-tuple-element.517, f32[4,512,4096]{2,1,0:T(8,128)} %fusion.195, f32[4,512,4096]{2,1,0:T(8,128)} %fusion.196, ...), kind=kOutput, calls=%fused_computation.52.clone.1 | convolution fusion | flops 1166022656 | bytes 141050368 | tf_op jit(solution)/shard_map/while/body/eval_jaxpr/hqk,khd->qhd/dot_general | solution.py:93
  938.3 18.5 %fusion.198 = f32[4096,4,64]{0,2,1:T(8,128)} fusion(f32[4,512,4096]{2,1,0:T(8,128)} %fusion.196, f32[4,512]{1,0:T(4,128)S(1)} %dynamic-slice_bitcast_fusion.2, pred[512,4096]{1,0:T(8,128)(4,1)} %compare_and_fusion.3, f32[4096,4,64]{0,2,1:T(8,128)} %get-tuple-element.499, pred[]{:T(512)S(6)} %compare.3, ...), kind=kOutput, calls=%fused_computation.50.clone.1 | convolution fusion | flops 1109393408 | bytes 44310532 | tf_op jit(solution)/shard_map/while/body/eval_jaxpr/hqk,qhd->khd/dot_general | solution.py:99
  956.9 5.6 copy.61
  962.7 5.6 copy.60
  973.7 6.6 fusion.118
  981.9 6.7 fusion.121
  992.0 47.7 %reduce-scatter.15.cloned.1.call-done = f32[1024,256]{1,0:T(8,128)} async-done(((f32[4096,256]{1,0:T(8,128)}), f32[1024,256]{1,0:T(8,128)}) %reduce-scatter.15.cloned.1.call-update) | async-done | bytes 1048592 | tf_op jit(solution)/shard_map/reduce_scatter | solution.py:184
  1040.9 78.2 %reduce-scatter.13.cloned.1.call-done = f32[1024,256]{1,0:T(8,128)} async-done(((f32[4096,256]{1,0:T(8,128)}), f32[1024,256]{1,0:T(8,128)}) %reduce-scatter.13.cloned.1.call-update) | async-done | bytes 1048592 | tf_op jit(solution)/shard_map/reduce_scatter | solution.py:181
  1128.1 5.3 convolution_bitcast_fusion
  1133.5 9.4 reduce-scatter.19.cloned.1.call-done
  1142.9 56.5 %reduce-scatter.23.cloned.1.call-done = f32[1024,512]{1,0:T(8,128)} async-done(((f32[1024,1024]{1,0:T(8,128)}), f32[1024,512]{1,0:T(8,128)}) %reduce-scatter.23.cloned.1.call-update) | async-done | bytes 2097168 | tf_op jit(solution)/shard_map/reduce_scatter | solution.py:204
  1199.4 56.7 %reduce-scatter.21.cloned.1.call-done = f32[512,1024]{1,0:T(8,128)} async-done(((f32[1024,1024]{1,0:T(8,128)}), f32[512,1024]{1,0:T(8,128)}) %reduce-scatter.21.cloned.1.call-update) | async-done | bytes 2097168 | tf_op jit(solution)/shard_map/reduce_scatter | solution.py:203
  1256.1 45.5 %reduce-scatter.17.cloned.1.call-done = f32[3,512,256]{1,2,0:T(8,128)} async-done(((f32[3,1024,256]{1,2,0:T(8,128)}), f32[3,512,256]{1,2,0:T(8,128)}) %reduce-scatter.17.cloned.1.call-update) | async-done | bytes 1572880 | tf_op jit(solution)/shard_map/reduce_scatter | solution.py:201
  1301.6 17.3 %reduce-scatter.25.cloned.1.call-done = f32[512,2]{1,0:T(8,128)} async-done(((f32[1024,2]{1,0:T(8,128)}), f32[512,2]{1,0:T(8,128)}) %reduce-scatter.25.cloned.1.call-update) | async-done | bytes 4112
  1320.0 16.2 reduce-scatter.27.cloned.1.call-done
  1337.2 12.4 all-reduce
  1349.7 74.4 %all-reduce.14.cloned.1.call-done = f32[1024,1024]{1,0:T(8,128)} async-done(((f32[1024,1024]{1,0:T(8,128)}), f32[1024,1024]{1,0:T(8,128)}) %all-reduce.14.cloned.1.call-update) | async-done | bytes 4194320 | tf_op jit(solution)/shard_map/psum | solution.py:36
  1424.0 5.2 add_convert_fusion
  1429.2 221.3 %all-reduce.16.cloned.1.call-done = (f32[3,512,256]{1,2,0:T(8,128)}, f32[256,512]{1,0:T(8,128)}, f32[512,1024]{1,0:T(8,128)}, f32[1024,512]{1,0:T(8,128)}) async-done(((f32[3,512,256]{1,2,0:T(8,128)}, f32[256,512]{1,0:T(8,128)}, f32[512,1024]{1,0:T(8,128)}, f32[1024,512]{1,0:T(8,128)}), (f32[3,512,256]{1,2,0:T(8,128)}, f32[256,512]{1,0:T(8,128)}, f32[512,1024]{1,0:T(8,128)}, ...) | async-done | bytes 6291472 | tf_op jit(solution)/shard_map/psum | solution.py:208
  (202 shorter events, 101.7 us)
Async XLA Ops:
  7.2 32.9 %all-gather.8.cloned.1.call-start = ((), (), s32[]{:S(2)}) async-start(), calls=%async_computation.8 | async-start | bytes 2359296 | tf_op jit(solution)/shard_map/all_gather | solution.py:111
  9.5 81.6 %all-gather.14.cloned.1.call-start = ((), (), s32[]{:S(2)}) async-start(), calls=%async_computation.21 | async-start | bytes 2621440 | tf_op jit(solution)/shard_map/all_gather | solution.py:133
  44.0 1.9 copy-start.37
  44.0 2.3 copy-start.16
  45.1 92.9 %all-gather.16.cloned.1.call-start = ((), (), s32[]{:S(2)}) async-start(), calls=%async_computation.22 | async-start | bytes 2621440 | tf_op jit(solution)/shard_map/all_gather | solution.py:134
  45.8 281.7 %all-reduce.8.cloned.1.call-start = ((), (), s32[]{:S(2)}) async-start(), calls=%async_computation.9 | async-start | bytes 8388608 | tf_op jit(solution)/shard_map/psum | solution.py:36
  138.0 102.4 %copy-start.11 = (bf16[256,1024]{1,0:T(8,128)(2,1)S(1)}, bf16[256,1024]{1,0:T(8,128)(2,1)}, u32[]{:S(2)}) copy-start(bf16[256,1024]{1,0:T(8,128)(2,1)} %all_gather.31) | copy-start | bytes 1572868
  243.1 5.6 copy-start.34
  243.1 84.4 %copy-start.9 = (bf16[1024,1024]{1,0:T(8,128)(2,1)S(1)}, bf16[1024,1024]{1,0:T(8,128)(2,1)}, u32[]{:S(2)}) copy-start(bf16[1024,1024]{1,0:T(8,128)(2,1)} %param.13) | copy-start | bytes 6291460
  243.2 119.1 %all-gather.10.cloned.1.call-start = ((), (), s32[]{:S(2)}) async-start(), calls=%async_computation.10 | async-start | bytes 3145728 | tf_op jit(solution)/shard_map/all_gather | solution.py:113
  243.7 153.1 %all-gather.12.cloned.1.call-start = ((), (), s32[]{:S(2)}) async-start(), calls=%async_computation.11 | async-start | bytes 3145728 | tf_op jit(solution)/shard_map/all_gather | solution.py:114
  244.3 244.7 %all-reduce.10.cloned.1.call-start = ((), (), s32[]{:S(2)}) async-start(), calls=%async_computation.12 | async-start | bytes 8388608 | tf_op jit(solution)/shard_map/psum | solution.py:36
  248.7 356.8 %copy-start.21 = (f32[1,1024]{1,0:T(1,128)}, f32[1,1024]{1,0:T(1,128)S(1)}, u32[]{:S(2)}) copy-start(f32[1,1024]{1,0:T(1,128)S(1)} %get-tuple-element.329) | copy-start | bytes 12292
  253.3 235.7 %copy-start.28 = (f32[1,1024]{1,0:T(1,128)}, f32[1,1024]{1,0:T(1,128)S(1)}, u32[]{:S(2)}) copy-start(f32[1,1024]{1,0:T(1,128)S(1)} %get-tuple-element.331) | copy-start | bytes 12292
  330.2 2.0 copy-start
  330.2 275.3 %copy-start.17 = (f32[1024]{0:T(1024)}, f32[1024]{0:T(1024)S(1)}, u32[]{:S(2)}) copy-start(f32[1024]{0:T(1024)S(1)} %broadcast_multiply_fusion.1) | copy-start | bytes 12292
  332.7 272.8 %copy-start.19 = (f32[1024]{0:T(1024)}, f32[1024]{0:T(1024)S(1)}, u32[]{:S(2)}) copy-start(f32[1024]{0:T(1024)S(1)} %fusion.114) | copy-start | bytes 12292
  403.4 195.7 %all-reduce.12.cloned.1.call-start = ((), (), s32[]{:S(2)}) async-start(), calls=%async_computation.13 | async-start | bytes 8388608 | tf_op jit(solution)/shard_map/psum | solution.py:36
  497.4 3.2 copy-start.36
  497.4 3.2 copy-start.38
  497.4 6.3 copy-start.39
  500.6 7.0 copy-start.5
  500.6 98.5 %copy-start.25 = (f32[1024]{0:T(1024)}, f32[1024]{0:T(1024)S(1)}, u32[]{:S(2)}) copy-start(f32[1024]{0:T(1024)S(1)} %negate_multiply_fusion.2) | copy-start | bytes 12292
  503.7 5.2 copy-start.35
  513.3 526.3 %reduce-scatter.15.cloned.1.call-start = ((), (), s32[]{:S(2)}) async-start(), calls=%async_computation.15 | async-start | bytes 5242880 | tf_op jit(solution)/shard_map/reduce_scatter | solution.py:184
  599.1 6.4 copy-start.1
  607.2 2.0 copy-start.4
  607.3 7.9 copy-start.23
  609.2 5.9 copy-start.2
  618.2 13.1 copy-start.3
  788.1 13.1 copy-start.3
  962.6 156.5 %reduce-scatter.13.cloned.1.call-start = ((), (), s32[]{:S(2)}) async-start(), calls=%async_computation.14 | async-start | bytes 5242880 | tf_op jit(solution)/shard_map/reduce_scatter | solution.py:181
  968.3 5.4 copy-start.26
  968.3 5.4 copy-start.40
  968.3 174.5 %reduce-scatter.19.cloned.1.call-start = ((), (), s32[]{:S(2)}) async-start(), calls=%async_computation.18 | async-start | bytes 1572864 | tf_op jit(solution)/shard_map/reduce_scatter | solution.py:202
  973.6 225.7 %reduce-scatter.23.cloned.1.call-start = ((), (), s32[]{:S(2)}) async-start(), calls=%async_computation.20 | async-start | bytes 6291456 | tf_op jit(solution)/shard_map/reduce_scatter | solution.py:204
  980.4 275.7 %reduce-scatter.21.cloned.1.call-start = ((), (), s32[]{:S(2)}) async-start(), calls=%async_computation.19 | async-start | bytes 6291456 | tf_op jit(solution)/shard_map/reduce_scatter | solution.py:203
  988.7 132.5 %copy-start.10 = (bf16[1024,1024]{1,0:T(8,128)(2,1)S(1)}, bf16[1024,1024]{1,0:T(8,128)(2,1)}, u32[]{:S(2)}) copy-start(bf16[1024,1024]{1,0:T(8,128)(2,1)} %param.13) | copy-start | bytes 6291460
  988.7 312.8 %reduce-scatter.17.cloned.1.call-start = ((), (), s32[]{:S(2)}) async-start(), calls=%async_computation.17 | async-start | bytes 4718592 | tf_op jit(solution)/shard_map/reduce_scatter | solution.py:201
  1121.2 4.6 copy-start.30
  1121.2 4.6 copy-start.32
  1125.7 2.4 copy-start.13
  1125.7 2.4 copy-start.15
  1125.8 193.1 %reduce-scatter.25.cloned.1.call-start = ((), (), s32[]{:S(2)}) async-start(), calls=%async_computation.23 | async-start | bytes 786432
  1126.9 209.2 %reduce-scatter.27.cloned.1.call-start = ((), (), s32[]{:S(2)}) async-start(), calls=%async_computation.24 | async-start | bytes 786432
  1128.0 296.0 %all-reduce.14.cloned.1.call-start = ((), (), s32[]{:S(2)}) async-start(), calls=%async_computation.16 | async-start | bytes 8388608 | tf_op jit(solution)/shard_map/psum | solution.py:36
  1133.4 517.1 %all-reduce.16.cloned.1.call-start = ((), (), s32[]{:S(2)}) async-start(), calls=%async_computation.25 | async-start | bytes 12582912 | tf_op jit(solution)/shard_map/psum | solution.py:208
  1650.5 8.2 copy-start.12
  (14 other events, 15.0 us)
Sparse Core Ops, SparseCore 0:
  10.1 29.8 all-gather.7
  45.2 45.9 all-gather.13
  93.3 44.6 all-gather.15
  243.3 84.1 all-reduce.7
  329.0 33.2 all-gather.9
  363.7 33.1 all-gather.11
  403.5 85.4 all-reduce.9
  513.5 85.6 all-reduce.11
  962.7 76.8 reduce-scatter.14
  1041.8 77.2 reduce-scatter.12
  1122.0 20.8 reduce-scatter.18
  1145.0 54.3 reduce-scatter.22
  1201.8 54.2 reduce-scatter.20
  1258.2 43.3 reduce-scatter.16
  1304.3 14.5 reduce-scatter.24
  1321.6 14.5 reduce-scatter.26
  1338.5 85.4 all-reduce.13
  1426.5 223.9 all-reduce.15
where the time goes:
time: 1670 us
  waiting for transfers between devices  1030 us (62%)
  matrix products  465 us (28%)
  other arithmetic  71.4 us (4%)
  local copies, waits for them, and re-layouts  51.7 us (3%)
  blocking collectives  30.3 us (2%)
    psum x4, waiting for transfers between devices, tp_total(): return lax.psum(terms, 'tp')  319 us
    psum x1, waiting for transfers between devices, body(): lax.psum((qkv_grad, out_proj_grad, up_grad, down_grad, gain_grad, shift_g...  221 us
    dot_general x2, matrix products, one_block(): jnp.einsum('hqk,qhd->khd', grad_scores, query_block, preferred_element_ty...  128 us
    dot_general x2, matrix products, one_block(): jnp.einsum('hqk,khd->qhd', grad_scores, key_heads, preferred_element_type...  120 us
    reduce_scatter x1, waiting for transfers between devices, body(): lax.psum_scatter(key_grad.reshape(pack_rows, local_width), 'ctx', scatter...  78.2 us
    dot_general x4, matrix products, score_block(): jnp.einsum('qhd,khd->hqk', query_block, key_heads, preferred_element_type...  57.8 us
    reduce_scatter x1, waiting for transfers between devices, body(): lax.psum_scatter(up_grad, 'fsdp', scatter_dimension=0, tiled=True)  56.7 us
    reduce_scatter x1, waiting for transfers between devices, body(): lax.psum_scatter(down_grad, 'fsdp', scatter_dimension=1, tiled=True)  56.5 us
  transfers between devices with their start and end apart: 18, of which 18 were waited for; matrix products, arithmetic and copies ran while one was open for 4% of the time, Pallas kernels for 0%

commit v1 on v0

--- a/solution.py
+++ b/solution.py
@@ -8,6 +8,27 @@
 SEQS = 3
 norm_eps = 1e-12
 masked_low = -1e30
+
+
+def collect(x, axis, dim):
+    size, mine, extent = (lax.axis_size(axis), lax.axis_index(axis), x.shape[dim])
+    right = [(i, (i + 1) % size) for i in range(size)]
+    behind = [(i, (i - 1) % size) for i in range(size)]
+    result = jnp.zeros((*x.shape[:dim], size * extent, *x.shape[dim + 1 :]), x.dtype)
+    result = lax.dynamic_update_slice_in_dim(result, x, mine * extent, axis=dim)
+    from_left = from_right = x
+    half = size // 2
+    for step in range(1, half + 1):
+        from_left = lax.ppermute(from_left, axis, right)
+        result = lax.dynamic_update_slice_in_dim(
+            result, from_left, (mine - step) % size * extent, axis=dim
+        )
+        if step < size - half:
+            from_right = lax.ppermute(from_right, axis, behind)
+            result = lax.dynamic_update_slice_in_dim(
+                result, from_right, (mine + step) % size * extent, axis=dim
+            )
+    return result
 
 
 def layer_norm(rows, gain, shift):
@@ -130,7 +151,7 @@
         "td,sdc->stc", tokens, full_qkv, preferred_element_type=jnp.float32
     ).astype(jnp.bfloat16)
     key_rows, value_rows = (
-        lax.all_gather(projected[1], "ctx", axis=0, tiled=True),
+        collect(projected[1], "ctx", 0),
         lax.all_gather(projected[2], "ctx", axis=0, tiled=True),
     )
     key_heads = key_rows.reshape(pack_rows, local_heads, HEAD_DIM)

time: 1670 us -> 1650 us (0.988)
  waiting for transfers between devices: 1030 us -> 991 us
    all_gather x1, waiting for transfers between devices: 46.9 us -> 5.14 us  [body(): lax.all_gather(projected[2], 'ctx', axis=0, tiled=True)]
    ppermute x0 -> x3, waiting for transfers between devices: none -> 36 us  [the longest x1 18.4 us: collect(): from_right = lax.ppermute(from_right, axis, behind)]
    all_gather x1 -> x0, waiting for transfers between devices: 35.5 us -> none  [body(): lax.all_gather(projected[1], 'ctx', axis=0, tiled=True)]
    unnamed x20 -> x19, waiting for transfers between devices: 35.5 us -> 34.8 us
  transfers between devices with their start and end apart: 18 -> 20, of which waited for: 18 -> 20; matrix products, arithmetic and copies ran while one was open for 4% -> 5% of each run, Pallas kernels for 0% -> 0%
where the time goes in v1:
time: 1650 us
  waiting for transfers between devices  991 us (60%)
  matrix products  468 us (28%)
  other arithmetic  71.4 us (4%)
  local copies, waits for them, and re-layouts  58.6 us (4%)
  blocking collectives  29.5 us (2%)
    psum x4, waiting for transfers between devices, tp_total(): return lax.psum(terms, 'tp')  321 us
    psum x1, waiting for transfers between devices, body(): lax.psum((qkv_grad, out_proj_grad, up_grad, down_grad, gain_grad, shift_g...  221 us
    dot_general x2, matrix products, one_block(): jnp.einsum('hqk,qhd->khd', grad_scores, query_block, preferred_element_ty...  127 us
    dot_general x2, matrix products, one_block(): jnp.einsum('hqk,khd->qhd', grad_scores, key_heads, preferred_element_type...  121 us
    reduce_scatter x1, waiting for transfers between devices, body(): lax.psum_scatter(key_grad.reshape(pack_rows, local_width), 'ctx', scatter...  78.3 us
    dot_general x4, matrix products, score_block(): jnp.einsum('qhd,khd->hqk', query_block, key_heads, preferred_element_type...  60.9 us
    reduce_scatter x1, waiting for transfers between devices, body(): lax.psum_scatter(down_grad, 'fsdp', scatter_dimension=1, tiled=True)  56.7 us
    reduce_scatter x1, waiting for transfers between devices, body(): lax.psum_scatter(up_grad, 'fsdp', scatter_dimension=0, tiled=True)  56.6 us
  transfers between devices with their start and end apart: 20, of which 20 were waited for; matrix products, arithmetic and copies ran while one was open for 5% of the time, Pallas kernels for 0%

profile of v1, /device:TPU:0, one launch (start us, length us, event | category | flops | bytes accessed | tf_op | source)
XLA Modules:
  0.0 1650.5 jit_solution(7366118310210114163)
XLA Ops:
  9.6 30.5 %all-gather.6.cloned.1.call-done = bf16[3,1024,256]{1,2,0:T(8,128)(2,1)} async-done(((bf16[3,512,256]{1,2,0:T(8,128)(2,1)}), bf16[3,1024,256]{1,2,0:T(8,128)(2,1)}) %all-gather.6.cloned.1.call-update) | async-done | bytes 1572880 | tf_op jit(solution)/shard_map/all_gather | solution.py:132
  49.0 8.3 all_gather.27
  57.4 9.0 collective-permute-done
  66.5 11.2 collective-permute-start.2
  81.5 18.4 %collective-permute-done.1 = bf16[1024,256]{0,1:T(8,128)(2,1)} collective-permute-done((bf16[1024,256]{0,1:T(8,128)(2,1)}, bf16[1024,256]{0,1:T(8,128)(2,1)}, u32[]{:S(2)}, u32[]{:S(2)}) %collective-permute-start.1) | collective-permute-done | bytes 524320 | tf_op jit(solution)/shard_map/ppermute | solution.py:27
  101.8 8.6 collective-permute-done.2
  117.4 99.8 %while.27 = (s32[]{:T(128)}, bf16[2,512,4,64]{1,3,2,0:T(8,128)(2,1)}, f32[2,4,512]{2,1,0:T(4,128)S(1)}, s32[2,512]{1,0:T(2,128)S(1)}, s32[4096]{0:T(1024)S(1)}, ...) while((s32[]{:T(128)}, ...), condition=%wide.region_6.7_spmd, body=%wide.region_2.6_spmd.sunk | while | flops 2271357440 | bytes 113924704 | solution.py:94
  119.7 15.8 fusion.181
  135.5 15.6 fusion.182
  151.1 16.2 fusion.183
  169.6 15.8 fusion.181
  185.4 15.6 fusion.182
  201.0 16.2 fusion.183
  232.6 75.3 %all-reduce.8.cloned.1.call-done = f32[1024,1024]{1,0:T(8,128)} async-done(((f32[1024,1024]{1,0:T(8,128)}), f32[1024,1024]{1,0:T(8,128)}) %all-reduce.8.cloned.1.call-update) | async-done | bytes 4194320 | tf_op jit(solution)/shard_map/psum | solution.py:57
  313.1 29.5 %all-gather.8.cloned.1.call-done = bf16[1024,1024]{1,0:T(8,128)(2,1)} async-done(((bf16[512,1024]{1,0:T(8,128)(2,1)}), bf16[1024,1024]{1,0:T(8,128)(2,1)}) %all-gather.8.cloned.1.call-update) | async-done | bytes 2097168 | tf_op jit(solution)/shard_map/all_gather | solution.py:134
  342.7 15.5 multiply_convert_fusion.1
  358.2 19.1 %all-gather.10.cloned.1.call-done = bf16[1024,1024]{1,0:T(8,128)(2,1)} async-done(((bf16[1024,512]{1,0:T(8,128)(2,1)}), bf16[1024,1024]{1,0:T(8,128)(2,1)}) %all-gather.10.cloned.1.call-update) | async-done | bytes 2097168 | tf_op jit(solution)/shard_map/all_gather | solution.py:135
  377.3 6.5 fusion.135
  384.3 85.2 %all-reduce.10.cloned.1.call-done = f32[1024,1024]{1,0:T(8,128)} async-done(((f32[1024,1024]{1,0:T(8,128)}), f32[1024,1024]{1,0:T(8,128)}) %all-reduce.10.cloned.1.call-update) | async-done | bytes 4194320 | tf_op jit(solution)/shard_map/psum | solution.py:57
  493.8 85.7 %all-reduce.12.cloned.1.call-done = f32[1024,1024]{1,0:T(8,128)} async-done(((f32[1024,1024]{1,0:T(8,128)}), f32[1024,1024]{1,0:T(8,128)}) %all-reduce.12.cloned.1.call-update) | async-done | bytes 4194320 | tf_op jit(solution)/shard_map/psum | solution.py:57
  579.5 6.4 multiply_reduce_fusion.1
  595.6 344.9 %while.28 = (s32[]{:T(128)}, f32[4096,4,64]{0,2,1:T(8,128)}, f32[4096,4,64]{0,2,1:T(8,128)}, bf16[2,512,4,64]{1,3,2,0:T(8,128)(2,1)}, bf16[2,512,4,64]{1,3,2,0:T...) while((s32[]{:T(128)}, f32[4096,4,64]{0,2,1:T(8,128)}, ...), condition=%wide.region_20.21_spmd.clone, body=%wide.region_18.20_spmd.clone.sunk | while | flops 5595217920 | bytes 406428800 | solution.py:125
  598.7 14.7 fusion.196
  613.3 13.1 fusion.195
  626.4 63.2 %fusion.197 = f32[4096,4,64]{0,2,1:T(8,128)} fusion(f32[4,512,4096]{2,1,0:T(8,128)} %fusion.195, f32[4,512,4096]{2,1,0:T(8,128)} %fusion.196, f32[4,512]{1,0:T(4,128)S(1)} %dynamic-slice_bitcast_fusion.2, pred[512,4096]{1,0:T(8,128)(4,1)} %compare_and_fusion.3, f32[4096,4,64]{0,2,1:T(8,128)} %get-tuple-element.498, pred[]{:T(512)S(6)} %compare.6, ...), kind=kOutput, calls=%fused_computation.48.clone.1 | convolution fusion | flops 1168119808 | bytes 147079680 | tf_op jit(solution)/shard_map/while/body/eval_jaxpr/hqk,qhd->khd/dot_general | solution.py:117
  689.6 60.3 %fusion.199 = bf16[2,512,4,64]{1,3,2,0:T(8,128)(2,1)} fusion(bf16[2,512,4,64]{1,3,2,0:T(8,128)(2,1)} %get-tuple-element.500, s32[]{:T(128)} %get-tuple-element.497, bf16[4096,4,64]{0,2,1:T(8,128)(2,1)} %get-tuple-element.517, f32[4,512,4096]{2,1,0:T(8,128)} %fusion.195, f32[4,512,4096]{2,1,0:T(8,128)} %fusion.196, ...), kind=kOutput, calls=%fused_computation.52.clone.1 | convolution fusion | flops 1166022656 | bytes 141050368 | tf_op jit(solution)/shard_map/while/body/eval_jaxpr/hqk,khd->qhd/dot_general | solution.py:114
  749.9 17.4 %fusion.198 = f32[4096,4,64]{0,2,1:T(8,128)} fusion(f32[4,512,4096]{2,1,0:T(8,128)} %fusion.196, f32[4,512]{1,0:T(4,128)S(1)} %dynamic-slice_bitcast_fusion.2, pred[512,4096]{1,0:T(8,128)(4,1)} %compare_and_fusion.3, f32[4096,4,64]{0,2,1:T(8,128)} %get-tuple-element.499, pred[]{:T(512)S(6)} %compare.6, ...), kind=kOutput, calls=%fused_computation.50.clone.1 | convolution fusion | flops 1109393408 | bytes 44310532 | tf_op jit(solution)/shard_map/while/body/eval_jaxpr/hqk,qhd->khd/dot_general | solution.py:120
  770.1 14.7 fusion.196
  784.8 13.1 fusion.195
  797.9 63.6 %fusion.197 = f32[4096,4,64]{0,2,1:T(8,128)} fusion(f32[4,512,4096]{2,1,0:T(8,128)} %fusion.195, f32[4,512,4096]{2,1,0:T(8,128)} %fusion.196, f32[4,512]{1,0:T(4,128)S(1)} %dynamic-slice_bitcast_fusion.2, pred[512,4096]{1,0:T(8,128)(4,1)} %compare_and_fusion.3, f32[4096,4,64]{0,2,1:T(8,128)} %get-tuple-element.498, pred[]{:T(512)S(6)} %compare.6, ...), kind=kOutput, calls=%fused_computation.48.clone.1 | convolution fusion | flops 1168119808 | bytes 147079680 | tf_op jit(solution)/shard_map/while/body/eval_jaxpr/hqk,qhd->khd/dot_general | solution.py:117
  861.5 60.3 %fusion.199 = bf16[2,512,4,64]{1,3,2,0:T(8,128)(2,1)} fusion(bf16[2,512,4,64]{1,3,2,0:T(8,128)(2,1)} %get-tuple-element.500, s32[]{:T(128)} %get-tuple-element.497, bf16[4096,4,64]{0,2,1:T(8,128)(2,1)} %get-tuple-element.517, f32[4,512,4096]{2,1,0:T(8,128)} %fusion.195, f32[4,512,4096]{2,1,0:T(8,128)} %fusion.196, ...), kind=kOutput, calls=%fused_computation.52.clone.1 | convolution fusion | flops 1166022656 | bytes 141050368 | tf_op jit(solution)/shard_map/while/body/eval_jaxpr/hqk,khd->qhd/dot_general | solution.py:114
  921.8 18.5 %fusion.198 = f32[4096,4,64]{0,2,1:T(8,128)} fusion(f32[4,512,4096]{2,1,0:T(8,128)} %fusion.196, f32[4,512]{1,0:T(4,128)S(1)} %dynamic-slice_bitcast_fusion.2, pred[512,4096]{1,0:T(8,128)(4,1)} %compare_and_fusion.3, f32[4096,4,64]{0,2,1:T(8,128)} %get-tuple-element.499, pred[]{:T(512)S(6)} %compare.6, ...), kind=kOutput, calls=%fused_computation.50.clone.1 | convolution fusion | flops 1109393408 | bytes 44310532 | tf_op jit(solution)/shard_map/while/body/eval_jaxpr/hqk,qhd->khd/dot_general | solution.py:120
  940.5 5.7 copy.61
  946.2 5.6 copy.60
  957.3 6.6 fusion.118
  965.5 6.8 fusion.121
  975.6 47.7 %reduce-scatter.15.cloned.1.call-done = f32[1024,256]{1,0:T(8,128)} async-done(((f32[4096,256]{1,0:T(8,128)}), f32[1024,256]{1,0:T(8,128)}) %reduce-scatter.15.cloned.1.call-update) | async-done | bytes 1048592 | tf_op jit(solution)/shard_map/reduce_scatter | solution.py:205
  1024.5 78.3 %reduce-scatter.13.cloned.1.call-done = f32[1024,256]{1,0:T(8,128)} async-done(((f32[4096,256]{1,0:T(8,128)}), f32[1024,256]{1,0:T(8,128)}) %reduce-scatter.13.cloned.1.call-update) | async-done | bytes 1048592 | tf_op jit(solution)/shard_map/reduce_scatter | solution.py:202
  1111.8 5.2 convolution_bitcast_fusion
  1117.1 9.3 reduce-scatter.19.cloned.1.call-done
  1126.4 56.7 %reduce-scatter.23.cloned.1.call-done = f32[1024,512]{1,0:T(8,128)} async-done(((f32[1024,1024]{1,0:T(8,128)}), f32[1024,512]{1,0:T(8,128)}) %reduce-scatter.23.cloned.1.call-update) | async-done | bytes 2097168 | tf_op jit(solution)/shard_map/reduce_scatter | solution.py:225
  1183.1 56.6 %reduce-scatter.21.cloned.1.call-done = f32[512,1024]{1,0:T(8,128)} async-done(((f32[1024,1024]{1,0:T(8,128)}), f32[512,1024]{1,0:T(8,128)}) %reduce-scatter.21.cloned.1.call-update) | async-done | bytes 2097168 | tf_op jit(solution)/shard_map/reduce_scatter | solution.py:224
  1239.6 45.6 %reduce-scatter.17.cloned.1.call-done = f32[3,512,256]{1,2,0:T(8,128)} async-done(((f32[3,1024,256]{1,2,0:T(8,128)}), f32[3,512,256]{1,2,0:T(8,128)}) %reduce-scatter.17.cloned.1.call-update) | async-done | bytes 1572880 | tf_op jit(solution)/shard_map/reduce_scatter | solution.py:222
  1285.3 17.3 %reduce-scatter.27.cloned.1.call-done = f32[512,2]{1,0:T(8,128)} async-done(((f32[1024,2]{1,0:T(8,128)}), f32[512,2]{1,0:T(8,128)}) %reduce-scatter.27.cloned.1.call-update) | async-done | bytes 4112
  1303.7 16.2 reduce-scatter.25.cloned.1.call-done
  1321.0 12.4 all-reduce
  1333.3 74.4 %all-reduce.14.cloned.1.call-done = f32[1024,1024]{1,0:T(8,128)} async-done(((f32[1024,1024]{1,0:T(8,128)}), f32[1024,1024]{1,0:T(8,128)}) %all-reduce.14.cloned.1.call-update) | async-done | bytes 4194320 | tf_op jit(solution)/shard_map/psum | solution.py:57
  1413.0 221.3 %all-reduce.16.cloned.1.call-done = (f32[3,512,256]{1,2,0:T(8,128)}, f32[256,512]{1,0:T(8,128)}, f32[512,1024]{1,0:T(8,128)}, f32[1024,512]{1,0:T(8,128)}) async-done(((f32[3,512,256]{1,2,0:T(8,128)}, f32[256,512]{1,0:T(8,128)}, f32[512,1024]{1,0:T(8,128)}, f32[1024,512]{1,0:T(8,128)}), (f32[3,512,256]{1,2,0:T(8,128)}, f32[256,512]{1,0:T(8,128)}, f32[512,1024]{1,0:T(8,128)}, ...) | async-done | bytes 6291472 | tf_op jit(solution)/shard_map/psum | solution.py:229
  (206 shorter events, 126.7 us)
Async XLA Ops:
  7.2 32.9 %all-gather.6.cloned.1.call-start = ((), (), s32[]{:S(2)}) async-start(), calls=%async_computation.8 | async-start | bytes 2359296 | tf_op jit(solution)/shard_map/all_gather | solution.py:132
  9.5 39.5 %copy-start.15 = (bf16[256,512]{1,0:T(8,128)(2,1)S(1)}, bf16[256,512]{1,0:T(8,128)(2,1)}, u32[]{:S(2)}) copy-start(bf16[256,512]{1,0:T(8,128)(2,1)} %param.15) | copy-start | bytes 786436
  9.5 107.9 %all-gather.12.cloned.1.call-start = ((), (), s32[]{:S(2)}) async-start(), calls=%async_computation.21 | async-start | bytes 2621440 | tf_op jit(solution)/shard_map/all_gather | solution.py:155
  44.0 13.3 copy-start.36
  45.1 262.8 %all-reduce.8.cloned.1.call-start = ((), (), s32[]{:S(2)}) async-start(), calls=%async_computation.9 | async-start | bytes 8388608 | tf_op jit(solution)/shard_map/psum | solution.py:57
  45.1 21.3 %collective-permute-start = (bf16[1024,256]{0,1:T(8,128)(2,1)}, bf16[1024,256]{0,1:T(8,128)(2,1)S(1)}, u32[]{:S(2)}, u32[]{:S(2)}) collective-permute-start(bf16[1024,256]{0,1:T(8,128)(2,1)} %get-tuple-element.326), channel_id=1, source_target_pairs={{0,4},{4,8},{8,12},{12,0},{1,5},{5,9},{9,13},{13,1},{2,6},{6,10},{... | collective-permute-start | bytes 1572872 | tf_op jit(solution)/shard_map/ppermute | solution.py:22
  46.7 53.3 %collective-permute-start.1 = (bf16[1024,256]{0,1:T(8,128)(2,1)}, bf16[1024,256]{0,1:T(8,128)(2,1)}, u32[]{:S(2)}, u32[]{:S(2)}) collective-permute-start(bf16[1024,256]{0,1:T(8,128)(2,1)} %get-tuple-element.326), channel_id=1, source_target_pairs={{0,12},{4,0},{8,4},{12,8},{1,13},{5,1},{9,5},{13,9},{2,14},{6,2},{... | collective-permute-start | bytes 1572872 | tf_op jit(solution)/shard_map/ppermute | solution.py:27
  66.5 43.9 %collective-permute-start.2 = (bf16[1024,256]{0,1:T(8,128)(2,1)S(1)}, bf16[1024,256]{0,1:T(8,128)(2,1)}, u32[]{:S(2)}, u32[]{:S(2)}) collective-permute-start(bf16[1024,256]{0,1:T(8,128)(2,1)S(1)} %collective-permute-done), channel_id=1, source_target_pairs={{0,4},{4,8},{8,12},{12,0},{1,5},{5,9},{9,13},{13,1},{2,6},{6,10},{... | collective-permute-start | bytes 1572872 | tf_op jit(solution)/shard_map/ppermute | solution.py:22
  117.4 102.3 %copy-start.10 = (bf16[256,1024]{1,0:T(8,128)(2,1)S(1)}, bf16[256,1024]{1,0:T(8,128)(2,1)}, u32[]{:S(2)}) copy-start(bf16[256,1024]{1,0:T(8,128)(2,1)} %all_gather.27) | copy-start | bytes 1572868
  222.4 5.6 copy-start.33
  222.4 85.5 %copy-start.8 = (bf16[1024,1024]{1,0:T(8,128)(2,1)S(1)}, bf16[1024,1024]{1,0:T(8,128)(2,1)}, u32[]{:S(2)}) copy-start(bf16[1024,1024]{1,0:T(8,128)(2,1)} %param.13) | copy-start | bytes 6291460
  222.5 120.2 %all-gather.8.cloned.1.call-start = ((), (), s32[]{:S(2)}) async-start(), calls=%async_computation.10 | async-start | bytes 3145728 | tf_op jit(solution)/shard_map/all_gather | solution.py:134
  223.1 154.2 %all-gather.10.cloned.1.call-start = ((), (), s32[]{:S(2)}) async-start(), calls=%async_computation.11 | async-start | bytes 3145728 | tf_op jit(solution)/shard_map/all_gather | solution.py:135
  223.6 245.8 %all-reduce.10.cloned.1.call-start = ((), (), s32[]{:S(2)}) async-start(), calls=%async_computation.12 | async-start | bytes 8388608 | tf_op jit(solution)/shard_map/psum | solution.py:57
  228.1 357.9 %copy-start.20 = (f32[1,1024]{1,0:T(1,128)}, f32[1,1024]{1,0:T(1,128)S(1)}, u32[]{:S(2)}) copy-start(f32[1,1024]{1,0:T(1,128)S(1)} %get-tuple-element.329) | copy-start | bytes 12292
  232.6 236.8 %copy-start.27 = (f32[1,1024]{1,0:T(1,128)}, f32[1,1024]{1,0:T(1,128)S(1)}, u32[]{:S(2)}) copy-start(f32[1,1024]{1,0:T(1,128)S(1)} %get-tuple-element.331) | copy-start | bytes 12292
  310.6 2.0 copy-start
  310.6 275.3 %copy-start.16 = (f32[1024]{0:T(1024)}, f32[1024]{0:T(1024)S(1)}, u32[]{:S(2)}) copy-start(f32[1024]{0:T(1024)S(1)} %broadcast_multiply_fusion.1) | copy-start | bytes 12292
  313.1 272.8 %copy-start.18 = (f32[1024]{0:T(1024)}, f32[1024]{0:T(1024)S(1)}, u32[]{:S(2)}) copy-start(f32[1024]{0:T(1024)S(1)} %fusion.114) | copy-start | bytes 12292
  383.8 195.7 %all-reduce.12.cloned.1.call-start = ((), (), s32[]{:S(2)}) async-start(), calls=%async_computation.13 | async-start | bytes 8388608 | tf_op jit(solution)/shard_map/psum | solution.py:57
  477.9 3.2 copy-start.35
  477.9 3.2 copy-start.37
  477.9 6.3 copy-start.38
  481.0 7.0 copy-start.4
  481.0 98.5 %copy-start.24 = (f32[1024]{0:T(1024)}, f32[1024]{0:T(1024)S(1)}, u32[]{:S(2)}) copy-start(f32[1024]{0:T(1024)S(1)} %negate_multiply_fusion.2) | copy-start | bytes 12292
  484.2 5.2 copy-start.34
  493.8 529.4 %reduce-scatter.15.cloned.1.call-start = ((), (), s32[]{:S(2)}) async-start(), calls=%async_computation.15 | async-start | bytes 5242880 | tf_op jit(solution)/shard_map/reduce_scatter | solution.py:205
  579.5 6.4 copy-start.1
  587.7 2.0 copy-start.3
  587.7 7.9 copy-start.22
  589.7 5.9 copy-start.2
  946.2 156.7 %reduce-scatter.13.cloned.1.call-start = ((), (), s32[]{:S(2)}) async-start(), calls=%async_computation.14 | async-start | bytes 5242880 | tf_op jit(solution)/shard_map/reduce_scatter | solution.py:202
  951.9 5.4 copy-start.25
  951.9 5.4 copy-start.39
  951.9 174.5 %reduce-scatter.19.cloned.1.call-start = ((), (), s32[]{:S(2)}) async-start(), calls=%async_computation.18 | async-start | bytes 1572864 | tf_op jit(solution)/shard_map/reduce_scatter | solution.py:223
  957.2 225.9 %reduce-scatter.23.cloned.1.call-start = ((), (), s32[]{:S(2)}) async-start(), calls=%async_computation.20 | async-start | bytes 6291456 | tf_op jit(solution)/shard_map/reduce_scatter | solution.py:225
  963.9 275.7 %reduce-scatter.21.cloned.1.call-start = ((), (), s32[]{:S(2)}) async-start(), calls=%async_computation.19 | async-start | bytes 6291456 | tf_op jit(solution)/shard_map/reduce_scatter | solution.py:224
  972.3 132.6 %copy-start.9 = (bf16[1024,1024]{1,0:T(8,128)(2,1)S(1)}, bf16[1024,1024]{1,0:T(8,128)(2,1)}, u32[]{:S(2)}) copy-start(bf16[1024,1024]{1,0:T(8,128)(2,1)} %param.13) | copy-start | bytes 6291460
  972.3 313.0 %reduce-scatter.17.cloned.1.call-start = ((), (), s32[]{:S(2)}) async-start(), calls=%async_computation.17 | async-start | bytes 4718592 | tf_op jit(solution)/shard_map/reduce_scatter | solution.py:222
  1104.9 4.6 copy-start.29
  1104.9 4.6 copy-start.31
  1109.4 2.4 copy-start.12
  1109.5 2.4 copy-start.14
  1109.5 193.1 %reduce-scatter.27.cloned.1.call-start = ((), (), s32[]{:S(2)}) async-start(), calls=%async_computation.23 | async-start | bytes 786432
  1110.6 209.3 %reduce-scatter.25.cloned.1.call-start = ((), (), s32[]{:S(2)}) async-start(), calls=%async_computation.22 | async-start | bytes 786432
  1111.8 296.0 %all-reduce.14.cloned.1.call-start = ((), (), s32[]{:S(2)}) async-start(), calls=%async_computation.16 | async-start | bytes 8388608 | tf_op jit(solution)/shard_map/psum | solution.py:57
  1117.1 517.2 %all-reduce.16.cloned.1.call-start = ((), (), s32[]{:S(2)}) async-start(), calls=%async_computation.24 | async-start | bytes 12582912 | tf_op jit(solution)/shard_map/psum | solution.py:229
  1634.3 8.2 copy-start.11
  (14 other events, 15.0 us)
Sparse Core Ops, SparseCore 0:
  10.1 29.8 all-gather.5
  45.2 72.1 all-gather.11
  222.6 85.2 all-reduce.7
  309.4 33.2 all-gather.7
  344.1 33.1 all-gather.9
  383.9 85.4 all-reduce.9
  493.9 85.6 all-reduce.11
  946.3 76.8 reduce-scatter.14
  1025.5 77.2 reduce-scatter.12
  1105.6 20.8 reduce-scatter.18
  1128.7 54.3 reduce-scatter.22
  1185.3 54.2 reduce-scatter.20
  1241.9 43.3 reduce-scatter.16
  1288.0 14.5 reduce-scatter.26
  1305.3 14.5 reduce-scatter.24
  1322.2 85.4 all-reduce.13
  1410.2 223.9 all-reduce.15
